TPU v7x, 512 devices: a whole 4x4x16 slice. The times are simulated.
512 devices in a mesh: seq: 128 (over y, z, core), head: 4 (over x).
Axes of the slice: x: 4, y: 4, z: 16, core: 2. Of those that a mesh axis runs over, the one named last changes fastest.
Arguments:
- queries: bfloat16 [65536, 2048], P('seq', 'head'), may hold values from -6 to 6
- key_vectors: bfloat16 [65536, 2048], P('seq', 'head'), may hold values from -6 to 6
- values: bfloat16 [65536, 2048], P('seq', 'head'), may hold values from -6 to 6
- out_weight: bfloat16 [2048, 2048], P('head', 'seq'), may hold values from -4 to 4
Outputs:
- mixed: bfloat16 [65536, 2048], P('seq', 'head')
All inputs are finite; a program needn't handle non-finite values.
Results may differ from a plain program's by a relative error of at most 0.0095.
Values may be sent and summed in bfloat16 or wider, within the bound.
No kernel may reach another device: no remote copies, remote signals or barrier semaphores. Data moves between devices by JAX's collectives and lax.ppermute only.
A program may use at most 64 MiB of HBM per device.

v0:
```python
import math
import jax
import jax.numpy as jnp
from jax import lax
from jax.sharding import PartitionSpec as P

HEAD_DIM = 128
BLOCK = 128
LEVELS = 5


def partner(value, axis, stride):
    mask = 2**stride
    pairs = [(source, source ^ mask) for source in range(lax.axis_size(axis))]
    return lax.ppermute(value, axis, pairs)


def pool_mean(array_in):
    paired = array_in.astype(jnp.float32).reshape(array_in.shape[0] // 2, 2, array_in.shape[1])
    return ((paired[:, 0] + paired[:, 1]) * 0.5).astype(jnp.bfloat16)


def pool_sum(array_in):
    paired = array_in.astype(jnp.float32).reshape(array_in.shape[0] // 2, 2, array_in.shape[1])
    return (paired[:, 0] + paired[:, 1]).astype(jnp.bfloat16)


def to_blocks(array_in, head_count, block_rows):
    return array_in.reshape(-1, block_rows, head_count, array_in.shape[1] // head_count)


def swap_pairs(blocked):
    block_count = blocked.shape[0]
    return blocked.reshape((block_count // 2, 2) + blocked.shape[1:])[:, ::-1].reshape(
        blocked.shape
    )


def level_terms(
    blocked_query_rows, blocked_key_rows, blocked_value_rows, weight, logit_scale_factor
):
    attention_logits = (
        jnp.einsum(
            "bqhd,bkhd->bhqk",
            blocked_query_rows,
            blocked_key_rows,
            preferred_element_type=jnp.float32,
        )
        * logit_scale_factor
    )
    peak_score = jnp.max(attention_logits, axis=-1)
    expo = jnp.exp(attention_logits - peak_score[..., None])
    mass = weight * jnp.sum(expo, axis=-1)
    weighted_value_sum = jnp.einsum(
        "bhqk,bkhd->bqhd",
        expo.astype(jnp.bfloat16),
        blocked_value_rows,
        preferred_element_type=jnp.float32,
    )
    head_count = blocked_query_rows.shape[2]
    peak_rows = jnp.transpose(peak_score, (0, 2, 1)).reshape(-1, head_count)
    mass_rows = jnp.transpose(mass, (0, 2, 1)).reshape(-1, head_count)
    return (
        peak_rows,
        mass_rows,
        weighted_value_sum.reshape(-1, head_count, weighted_value_sum.shape[3]),
    )


def merge_level(running, terms, factor):
    running_max, running_sum, running_out = running
    peak_rows = jnp.repeat(terms[0], factor, axis=0)
    mass_rows = jnp.repeat(terms[1], factor, axis=0)
    weighted_value_sum = jnp.repeat(terms[2], factor, axis=0)
    newest = jnp.maximum(running_max, peak_rows)
    keep_old = jnp.exp(running_max - newest)
    keep_new = jnp.exp(peak_rows - newest)
    return (
        newest,
        running_sum * keep_old + mass_rows * keep_new,
        running_out * keep_old[..., None] + weighted_value_sum * keep_new[..., None],
    )


def body(queries, key_vectors, values, out_weight):
    row_count, col_count = queries.shape
    head_count = col_count // HEAD_DIM
    logit_scale_factor = 1.0 / math.sqrt(HEAD_DIM)
    seq_index = lax.axis_index("seq")
    blocked_key_rows = to_blocks(key_vectors, head_count, BLOCK)
    blocked_value_rows = to_blocks(values, head_count, BLOCK)
    near_keys = jnp.concatenate([blocked_key_rows, swap_pairs(blocked_key_rows)], axis=1)
    near_values = jnp.concatenate([blocked_value_rows, swap_pairs(blocked_value_rows)], axis=1)
    running = level_terms(
        to_blocks(queries, head_count, BLOCK), near_keys, near_values, 1.0, logit_scale_factor
    )
    level_queries, level_keys, level_values = (queries, key_vectors, values)
    far_keys, far_values = (key_vectors, values)
    is_local = True
    partner_bit = 0
    for coarse_level in range(1, LEVELS + 1):
        level_queries = pool_mean(level_queries)
        if is_local:
            level_keys = pool_mean(level_keys)
            level_values = pool_sum(level_values)
            is_local = level_keys.shape[0] >= 2 * BLOCK
        else:
            leading = seq_index >> partner_bit - 1 & 1 == 0
            level_keys = pool_mean(
                jnp.concatenate(
                    [
                        jnp.where(leading, level_keys, far_keys),
                        jnp.where(leading, far_keys, level_keys),
                    ],
                    axis=0,
                )
            )
            level_values = pool_sum(
                jnp.concatenate(
                    [
                        jnp.where(leading, level_values, far_values),
                        jnp.where(leading, far_values, level_values),
                    ],
                    axis=0,
                )
            )
        if is_local:
            blocked_key_rows = swap_pairs(to_blocks(level_keys, head_count, BLOCK))
            blocked_value_rows = swap_pairs(to_blocks(level_values, head_count, BLOCK))
        else:
            far_keys, far_values = partner((level_keys, level_values), "seq", partner_bit)
            partner_bit += 1
            blocked_key_rows = to_blocks(far_keys, head_count, BLOCK)
            blocked_value_rows = to_blocks(far_values, head_count, BLOCK)
        blocked_query_rows = to_blocks(
            level_queries, head_count, level_queries.shape[0] // blocked_key_rows.shape[0]
        )
        terms = level_terms(
            blocked_query_rows,
            blocked_key_rows,
            blocked_value_rows,
            2.0**coarse_level,
            logit_scale_factor,
        )
        running = merge_level(running, terms, 2**coarse_level)
    attended = (
        (running[2] / running[1][..., None]).reshape(row_count, col_count).astype(jnp.bfloat16)
    )
    partial_terms = jnp.dot(
        attended,
        lax.all_gather(out_weight, "seq", axis=1, tiled=True),
        preferred_element_type=jnp.float32,
    )
    rounded_terms = partial_terms.astype(jnp.bfloat16).astype(jnp.float32)
    mixed = lax.psum_scatter(
        rounded_terms.astype(jnp.bfloat16), "head", scatter_dimension=1, tiled=True
    )
    return mixed


def solution(mesh):
    in_specs = (P("seq", "head"), P("seq", "head"), P("seq", "head"), P("head", "seq"))
    out_specs = P("seq", "head")
    return jax.shard_map(body, mesh=mesh, in_specs=in_specs, out_specs=out_specs, check_vma=False)
```

profile of v0, /device:TPU:1, one launch (start us, length us, event | category | flops | bytes accessed | tf_op | source)
XLA Modules:
  0.0 223.5 jit_solution(2739491692825542733)
XLA Ops:
  7.3 1.7 reshape.785
  10.7 8.7 %collective-permute-start = (bf16[128,512]{1,0:T(8,128)(2,1)S(1)}, bf16[128,512]{1,0:T(8,128)(2,1)}, u32[]{:S(2)}, u32[]{:S(2)}) collective-permute-start(bf16[128,512]{1,0:T(8,128)(2,1)S(1)} %fusion.53), channel_id=1, source_target_pairs={{0,4},{4,0},{8,12},{12,8},{16,20},{20,16},{24,28},{28,24},{32,36},... | collective-permute-start | bytes 393224 | tf_op jit(solution)/shard_map/ppermute | solution.py:15
  22.6 2.2 collective-permute-start.1
  33.2 1.0 copy.283
  35.3 1.1 convert_reduce_fusion.1
  39.2 1.0 fusion.1
  43.9 1.0 copy.311
  47.0 1.0 copy.317
  48.4 1.7 broadcast_select_fusion.9
  51.0 1.9 collective-permute-start.3
  52.9 1.0 maximum_convert_fusion
  54.6 3.6 %collective-permute-start.2 = (bf16[128,512]{1,0:T(8,128)(2,1)S(1)}, bf16[128,512]{1,0:T(8,128)(2,1)}, u32[]{:S(2)}, u32[]{:S(2)}) collective-permute-start(bf16[128,512]{1,0:T(8,128)(2,1)S(1)} %fusion.54), channel_id=1, source_target_pairs={{0,8},{4,12},{8,0},{12,4},{16,24},{20,28},{24,16},{28,20},{32,40},... | collective-permute-start | bytes 393224 | tf_op jit(solution)/shard_map/ppermute | solution.py:15
  59.1 1.9 collective-permute-start.5
  61.3 1.0 copy.323
  62.3 1.1 fusion.115
  67.5 4.0 %collective-permute-start.4 = (bf16[128,512]{1,0:T(8,128)(2,1)S(1)}, bf16[128,512]{1,0:T(8,128)(2,1)}, u32[]{:S(2)}, u32[]{:S(2)}) collective-permute-start(bf16[128,512]{1,0:T(8,128)(2,1)S(1)} %fusion.55), channel_id=1, source_target_pairs={{0,16},{4,20},{8,24},{12,28},{16,0},{20,4},{24,8},{28,12},{32,48},... | collective-permute-start | bytes 393224 | tf_op jit(solution)/shard_map/ppermute | solution.py:15
  71.5 1.3 fusion.99
  75.1 5.7 %collective-permute-start.7 = (bf16[128,512]{1,0:T(8,128)(2,1)}, bf16[128,512]{1,0:T(8,128)(2,1)}, u32[]{:S(2)}, u32[]{:S(2)}) collective-permute-start(bf16[128,512]{1,0:T(8,128)(2,1)} %bitcast.335), channel_id=1, source_target_pairs={{0,32},{4,36},{8,40},{12,44},{16,48},{20,52},{24,56},{28,60},{32,0... | collective-permute-start | bytes 393224 | tf_op jit(solution)/shard_map/ppermute | solution.py:15
  80.8 1.0 copy.341
  81.8 1.0 copy.335
  82.9 1.0 fusion.114
  87.5 3.5 %collective-permute-start.6 = (bf16[128,512]{1,0:T(8,128)(2,1)S(1)}, bf16[128,512]{1,0:T(8,128)(2,1)S(1)}, u32[]{:S(2)}, u32[]{:S(2)}) collective-permute-start(bf16[128,512]{1,0:T(8,128)(2,1)S(1)} %fusion.56), channel_id=1, source_target_pairs={{0,32},{4,36},{8,40},{12,44},{16,48},{20,52},{24,56},{28,60},{32,0... | collective-permute-start | bytes 393224 | tf_op jit(solution)/shard_map/ppermute | solution.py:15
  91.4 3.5 %collective-permute-done.7 = bf16[128,512]{1,0:T(8,128)(2,1)} collective-permute-done((bf16[128,512]{1,0:T(8,128)(2,1)}, bf16[128,512]{1,0:T(8,128)(2,1)}, u32[]{:S(2)}, u32[]{:S(2)}) %collective-permute-start.7) | collective-permute-done | bytes 131104 | tf_op jit(solution)/shard_map/ppermute | solution.py:15
  94.9 1.0 copy.351
  95.9 11.2 %collective-permute-done.6 = bf16[128,512]{1,0:T(8,128)(2,1)S(1)} collective-permute-done((bf16[128,512]{1,0:T(8,128)(2,1)S(1)}, bf16[128,512]{1,0:T(8,128)(2,1)S(1)}, u32[]{:S(2)}, u32[]{:S(2)}) %collective-permute-start.6) | collective-permute-done | bytes 131104 | tf_op jit(solution)/shard_map/ppermute | solution.py:15
  111.2 1.6 copy.297
  112.8 1.6 copy.314
  114.3 1.6 copy.326
  117.6 53.3 %all-gather.2.cloned.1.call-done = bf16[512,2048]{0,1:T(8,128)(2,1)} async-done(((bf16[512,16]{0,1:T(8,128)(2,1)}), bf16[512,2048]{0,1:T(8,128)(2,1)}) %all-gather.2.cloned.1.call-update) | async-done | bytes 2097168 | tf_op jit(solution)/shard_map/all_gather | solution.py:151
  171.1 1.6 mul.426
  179.8 3.5 %convolution_convert_fusion = bf16[512,2048]{1,0:T(8,128)(2,1)} fusion(bf16[512,2048]{0,1:T(8,128)(2,1)S(1)} %copy-done.2, f32[64,8,4,128]{3,2,1,0:T(4,128)S(1)} %bitcast.346, f32[64,8,4,128]{3,2,1,0:T(4,128)S(1)} %bitcast.341, f32[64,8,4,128]{3,2,1,0:T(4,128)S(1)} %bitcast.351, f32[64,8,4,128]{3,2,1,0:T(4,128)S(1)} %bitcast.336, ...), kind=kOutput, calls=%fused_computation | convolution fusion | flops 1079246848 | bytes 21102592 | tf_op jit(solution)/shard_map/dot_general | solution.py:149
  183.4 33.3 %reduce-scatter.2.cloned.1.call-done = bf16[512,512]{1,0:T(8,128)(2,1)} async-done(((bf16[512,2048]{1,0:T(8,128)(2,1)}), bf16[512,512]{1,0:T(8,128)(2,1)}) %reduce-scatter.2.cloned.1.call-update) | async-done | bytes 524304 | tf_op jit(solution)/shard_map/reduce_scatter | solution.py:155
  (215 shorter events, 49.0 us)
Async XLA Ops:
  6.5 164.4 %all-gather.2.cloned.1.call-start = ((), (), s32[]{:S(2)}) async-start(), calls=%async_computation.1 | async-start | bytes 2113536 | tf_op jit(solution)/shard_map/all_gather | solution.py:151
  7.3 209.4 %reduce-scatter.2.cloned.1.call-start = ((), (), s32[]{:S(2)}) async-start(), calls=%async_computation.2 | async-start | bytes 2621440 | tf_op jit(solution)/shard_map/reduce_scatter | solution.py:155
  9.8 9.7 %copy-start.1 = (bf16[512,512]{1,0:T(8,128)(2,1)S(1)}, bf16[512,512]{1,0:T(8,128)(2,1)}, u32[]{:S(2)}) copy-start(bf16[512,512]{1,0:T(8,128)(2,1)} %param.6) | copy-start | bytes 1572868
  10.7 33.1 %collective-permute-start = (bf16[128,512]{1,0:T(8,128)(2,1)S(1)}, bf16[128,512]{1,0:T(8,128)(2,1)}, u32[]{:S(2)}, u32[]{:S(2)}) collective-permute-start(bf16[128,512]{1,0:T(8,128)(2,1)S(1)} %fusion.53), channel_id=1, source_target_pairs={{0,4},{4,0},{8,12},{12,8},{16,20},{20,16},{24,28},{28,24},{32,36},... | collective-permute-start | bytes 393224 | tf_op jit(solution)/shard_map/ppermute | solution.py:15
  21.0 3.8 %copy-start = (bf16[512,512]{1,0:T(8,128)(2,1)S(1)}, bf16[512,512]{1,0:T(8,128)(2,1)}, u32[]{:S(2)}) copy-start(bf16[512,512]{1,0:T(8,128)(2,1)} %param.5) | copy-start | bytes 1572868
  22.6 4.4 %copy-start.3 = (bf16[512,512]{1,0:T(8,128)(2,1)S(1)}, bf16[512,512]{1,0:T(8,128)(2,1)}, u32[]{:S(2)}) copy-start(bf16[512,512]{1,0:T(8,128)(2,1)} %param.4) | copy-start | bytes 1572868
  22.6 24.5 %collective-permute-start.1 = (bf16[128,512]{1,0:T(8,128)(2,1)}, bf16[128,512]{1,0:T(8,128)(2,1)}, u32[]{:S(2)}, u32[]{:S(2)}) collective-permute-start(bf16[128,512]{1,0:T(8,128)(2,1)} %fusion.50), channel_id=1, source_target_pairs={{0,4},{4,0},{8,12},{12,8},{16,20},{20,16},{24,28},{28,24},{32,36},... | collective-permute-start | bytes 393224 | tf_op jit(solution)/shard_map/ppermute | solution.py:15
  29.3 3.0 %copy-start.4 = (bf16[2,2,128,4,128]{4,3,2,1,0:T(4,128)(2,1)S(1)}, bf16[2,2,128,4,128]{4,3,2,1,0:T(4,128)(2,1)}, u32[]{:S(2)}) copy-start(bf16[2,2,128,4,128]{4,3,2,1,0:T(4,128)(2,1)} %reshape_reshape.9) | copy-start | bytes 1572868
  34.6 3.1 %copy-start.11 = (bf16[1,2,128,4,128]{4,3,2,1,0:T(4,128)(2,1)S(1)}, bf16[1,2,128,4,128]{4,3,2,1,0:T(4,128)(2,1)}, u32[]{:S(2)}) copy-start(bf16[1,2,128,4,128]{4,3,2,1,0:T(4,128)(2,1)} %convert_element_type.246) | copy-start | bytes 786436
  34.6 3.2 %copy-start.12 = (bf16[2,128,4,128]{3,2,1,0:T(4,128)(2,1)S(1)}, bf16[2,128,4,128]{3,2,1,0:T(4,128)(2,1)}, u32[]{:S(2)}) copy-start(bf16[2,128,4,128]{3,2,1,0:T(4,128)(2,1)} %convert_element_type.244) | copy-start | bytes 786436
  51.0 7.3 %collective-permute-start.3 = (bf16[128,512]{1,0:T(8,128)(2,1)S(1)}, bf16[128,512]{1,0:T(8,128)(2,1)S(1)}, u32[]{:S(2)}, u32[]{:S(2)}) collective-permute-start(bf16[128,512]{1,0:T(8,128)(2,1)S(1)} %fusion.51), channel_id=1, source_target_pairs={{0,8},{4,12},{8,0},{12,4},{16,24},{20,28},{24,16},{28,20},{32,40},... | collective-permute-start | bytes 393224 | tf_op jit(solution)/shard_map/ppermute | solution.py:15
  54.6 6.6 %collective-permute-start.2 = (bf16[128,512]{1,0:T(8,128)(2,1)S(1)}, bf16[128,512]{1,0:T(8,128)(2,1)}, u32[]{:S(2)}, u32[]{:S(2)}) collective-permute-start(bf16[128,512]{1,0:T(8,128)(2,1)S(1)} %fusion.54), channel_id=1, source_target_pairs={{0,8},{4,12},{8,0},{12,4},{16,24},{20,28},{24,16},{28,20},{32,40},... | collective-permute-start | bytes 393224 | tf_op jit(solution)/shard_map/ppermute | solution.py:15
  59.1 13.7 %collective-permute-start.5 = (bf16[128,512]{1,0:T(8,128)(2,1)S(1)}, bf16[128,512]{1,0:T(8,128)(2,1)}, u32[]{:S(2)}, u32[]{:S(2)}) collective-permute-start(bf16[128,512]{1,0:T(8,128)(2,1)S(1)} %fusion.52), channel_id=1, source_target_pairs={{0,16},{4,20},{8,24},{12,28},{16,0},{20,4},{24,8},{28,12},{32,48},... | collective-permute-start | bytes 393224 | tf_op jit(solution)/shard_map/ppermute | solution.py:15
  67.5 14.4 %collective-permute-start.4 = (bf16[128,512]{1,0:T(8,128)(2,1)S(1)}, bf16[128,512]{1,0:T(8,128)(2,1)}, u32[]{:S(2)}, u32[]{:S(2)}) collective-permute-start(bf16[128,512]{1,0:T(8,128)(2,1)S(1)} %fusion.55), channel_id=1, source_target_pairs={{0,16},{4,20},{8,24},{12,28},{16,0},{20,4},{24,8},{28,12},{32,48},... | collective-permute-start | bytes 393224 | tf_op jit(solution)/shard_map/ppermute | solution.py:15
  75.1 19.7 %collective-permute-start.7 = (bf16[128,512]{1,0:T(8,128)(2,1)}, bf16[128,512]{1,0:T(8,128)(2,1)}, u32[]{:S(2)}, u32[]{:S(2)}) collective-permute-start(bf16[128,512]{1,0:T(8,128)(2,1)} %bitcast.335), channel_id=1, source_target_pairs={{0,32},{4,36},{8,40},{12,44},{16,48},{20,52},{24,56},{28,60},{32,0... | collective-permute-start | bytes 393224 | tf_op jit(solution)/shard_map/ppermute | solution.py:15
  83.9 2.6 %copy-start.22 = (f32[4,32]{1,0:T(4,128)}, f32[4,32]{1,0:T(4,128)S(1)}, u32[]{:S(2)}) copy-start(f32[4,32]{1,0:T(4,128)S(1)} %get-tuple-element.60) | copy-start | bytes 1540
  86.5 20.7 %copy-start.20 = (bf16[16,512]{1,0:T(8,128)(2,1)S(1)}, bf16[16,512]{1,0:T(8,128)(2,1)}, u32[]{:S(2)}) copy-start(bf16[16,512]{1,0:T(8,128)(2,1)} %convert_reduce_fusion.4) | copy-start | bytes 49156
  86.6 4.4 %copy-start.23 = (f32[4,32]{1,0:T(4,128)S(1)}, f32[4,32]{1,0:T(4,128)}, u32[]{:S(2)}) copy-start(f32[4,32]{1,0:T(4,128)} %copy-done.22) | copy-start | bytes 1540
  86.6 22.2 %copy-start.18 = (f32[512,4]{0,1:T(4,128)S(1)}, f32[512,4]{0,1:T(4,128)}, u32[]{:S(2)}) copy-start(f32[512,4]{0,1:T(4,128)} %reshape.749) | copy-start | bytes 24580
  86.6 22.2 %copy-start.19 = (f32[512,4]{0,1:T(4,128)S(1)}, f32[512,4]{0,1:T(4,128)}, u32[]{:S(2)}) copy-start(f32[512,4]{0,1:T(4,128)} %reshape.755) | copy-start | bytes 24580
  86.6 22.2 %copy-start.21 = (f32[4,4,128]{2,1,0:T(4,128)S(1)}, f32[4,4,128]{2,1,0:T(4,128)}, u32[]{:S(2)}) copy-start(f32[4,4,128]{2,1,0:T(4,128)} %fusion.1) | copy-start | bytes 24580
  86.6 22.2 %copy-start.24 = (f32[512,4]{0,1:T(4,128)S(1)}, f32[512,4]{0,1:T(4,128)}, u32[]{:S(2)}) copy-start(f32[512,4]{0,1:T(4,128)} %copy.356) | copy-start | bytes 24580
  86.6 22.2 %copy-start.25 = (f32[512,4]{0,1:T(4,128)S(1)}, f32[512,4]{0,1:T(4,128)}, u32[]{:S(2)}) copy-start(f32[512,4]{0,1:T(4,128)} %reshape.775) | copy-start | bytes 24580
  87.0 21.9 %copy-start.26 = (f32[512,4]{0,1:T(4,128)S(1)}, f32[512,4]{0,1:T(4,128)}, u32[]{:S(2)}) copy-start(f32[512,4]{0,1:T(4,128)} %reshape.777) | copy-start | bytes 24580
  87.0 21.9 %copy-start.27 = (f32[512,4]{0,1:T(4,128)S(1)}, f32[512,4]{0,1:T(4,128)}, u32[]{:S(2)}) copy-start(f32[512,4]{0,1:T(4,128)} %reshape.761) | copy-start | bytes 24580
  87.0 21.9 %copy-start.30 = (f32[512,4]{0,1:T(4,128)S(1)}, f32[512,4]{0,1:T(4,128)}, u32[]{:S(2)}) copy-start(f32[512,4]{0,1:T(4,128)} %get-tuple-element.18) | copy-start | bytes 24580
  87.0 21.9 %copy-start.31 = (f32[512,4]{0,1:T(4,128)S(1)}, f32[512,4]{0,1:T(4,128)}, u32[]{:S(2)}) copy-start(f32[512,4]{0,1:T(4,128)} %get-tuple-element.19) | copy-start | bytes 24580
  87.5 19.6 %collective-permute-start.6 = (bf16[128,512]{1,0:T(8,128)(2,1)S(1)}, bf16[128,512]{1,0:T(8,128)(2,1)S(1)}, u32[]{:S(2)}, u32[]{:S(2)}) collective-permute-start(bf16[128,512]{1,0:T(8,128)(2,1)S(1)} %fusion.56), channel_id=1, source_target_pairs={{0,32},{4,36},{8,40},{12,44},{16,48},{20,52},{24,56},{28,60},{32,0... | collective-permute-start | bytes 393224 | tf_op jit(solution)/shard_map/ppermute | solution.py:15
  109.6 6.3 %copy-start.29 = (f32[512,4]{0,1:T(4,128)S(1)}, f32[512,4]{0,1:T(4,128)}, u32[]{:S(2)}) copy-start(f32[512,4]{0,1:T(4,128)} %get-tuple-element.14) | copy-start | bytes 24580
  109.6 7.2 %copy-start.28 = (f32[512,4]{0,1:T(4,128)S(1)}, f32[512,4]{0,1:T(4,128)}, u32[]{:S(2)}) copy-start(f32[512,4]{0,1:T(4,128)} %get-tuple-element.15) | copy-start | bytes 24580
  170.9 2.4 %copy-start.9 = (f32[512,4]{1,0:T(8,128)S(1)}, f32[512,4]{1,0:T(8,128)}, u32[]{:S(2)}) copy-start(f32[512,4]{1,0:T(8,128)} %copy.326) | copy-start | bytes 24580
  171.1 2.8 %copy-start.8 = (f32[512,4]{1,0:T(8,128)S(1)}, f32[512,4]{1,0:T(8,128)}, u32[]{:S(2)}) copy-start(f32[512,4]{1,0:T(8,128)} %copy.314) | copy-start | bytes 24580
  (10 other events, 16.5 us)
Sparse Core Ops, SparseCore 0:
  10.5 160.4 all-gather.1
  183.5 33.1 reduce-scatter.1
where the time goes:
time: 224 us; the launch traced here: 223 us
  waiting for transfers between devices  102 us (46%)
  local copies, waits for them, and re-layouts  52.1 us (23%)
  starting transfers between devices  31.7 us (14%)
  between operations  14.6 us (7%)
  other arithmetic  14.2 us (6%)
  matrix products  8.56 us (4%)
    all_gather x1, waiting for transfers between devices, body(): lax.all_gather(out_weight, 'seq', axis=1, tiled=True)  53.3 us
    reduce_scatter x1, waiting for transfers between devices, body(): lax.psum_scatter(rounded_terms.astype(jnp.bfloat16), 'head', scatter_dime...  33.3 us
    ppermute x8, starting transfers between devices, partner(): return lax.ppermute(value, axis, pairs)  31.6 us
    ppermute x8, waiting for transfers between devices, partner(): return lax.ppermute(value, axis, pairs)  15 us
    exp x5, local copies, waits for them, and re-layouts, merge_level(): keep_old = jnp.exp(running_max - newest)  6.4 us
    ppermute x8, local copies, waits for them, and re-layouts, partner(): return lax.ppermute(value, axis, pairs)  6.36 us
  transfers between devices with their start and end apart: 10, of which 5 were waited for; matrix products, arithmetic and copies ran while one was open for 28% of the time, Pallas kernels for 0%

commit v1 on v0

--- a/solution.py
+++ b/solution.py
@@ -148,7 +148,9 @@
     )
     partial_terms = jnp.dot(
         attended,
-        lax.all_gather(out_weight, "seq", axis=1, tiled=True),
+        jnp.concatenate(
+            lax.all_to_all(jnp.stack([out_weight] * lax.axis_size("seq")), "seq", 0, 0), axis=1
+        ),
         preferred_element_type=jnp.float32,
     )
     rounded_terms = partial_terms.astype(jnp.bfloat16).astype(jnp.float32)

time: 224 us -> 238 us (1.062)
  starting transfers between devices: 31.7 us -> 48.6 us
  local copies, waits for them, and re-layouts: 52.1 us -> 35.9 us
  waiting for transfers between devices: 102 us -> 113 us
    ppermute x8, waiting for transfers between devices: 15 us -> 74.8 us  [partner(): return lax.ppermute(value, axis, pairs)]
    all_gather x1 -> x0, waiting for transfers between devices: 53.3 us -> none  [body(): lax.all_gather(out_weight, 'seq', axis=1, tiled=True)]
    all_to_all x0 -> x1, starting transfers between devices: none -> 14.8 us  [body(): lax.all_to_all(jnp.stack([out_weight] * lax.axis_size('seq')), 'seq', 0, 0)]
    exp x10 -> x0, local copies, waits for them, and re-layouts: 7.84 us -> none  [the longest x5 6.4 us: merge_level(): keep_old = jnp.exp(running_max - newest)]
    mul x10 -> x0, local copies, waits for them, and re-layouts: 7.01 us -> none  [the longest x5 3.99 us: merge_level(): running_out * keep_old[..., None] + weighted_value_sum * keep_new[..., None]]
    reduce_scatter x1, waiting for transfers between devices: 33.3 us -> 38.4 us  [body(): lax.psum_scatter(rounded_terms.astype(jnp.bfloat16), 'head', scatter_dime...]
    convert_element_type x0 -> x1, other arithmetic: none -> 3.77 us  [body(): (running[2] / running[1][..., None]).reshape(row_count, col_count)]
  transfers between devices with their start and end apart: 10 -> 10, of which waited for: 5 -> 3; matrix products, arithmetic and copies ran while one was open for 28% -> 22% of each run, Pallas kernels for 0% -> 0%
where the time goes in v1:
time: 238 us; the launch traced here: 237 us
  waiting for transfers between devices  113 us (47%)
  starting transfers between devices  48.6 us (20%)
  local copies, waits for them, and re-layouts  35.9 us (15%)
  other arithmetic  16.4 us (7%)
  between operations  14.5 us (6%)
  matrix products  8.55 us (4%)
    ppermute x8, waiting for transfers between devices, partner(): return lax.ppermute(value, axis, pairs)  74.8 us
    reduce_scatter x1, waiting for transfers between devices, body(): lax.psum_scatter(rounded_terms.astype(jnp.bfloat16), 'head', scatter_dime...  38.4 us
    ppermute x8, starting transfers between devices, partner(): return lax.ppermute(value, axis, pairs)  33.6 us
    all_to_all x1, starting transfers between devices, body(): lax.all_to_all(jnp.stack([out_weight] * lax.axis_size('seq')), 'seq', 0, 0)  14.8 us
    ppermute x8, local copies, waits for them, and re-layouts, partner(): return lax.ppermute(value, axis, pairs)  6.36 us
  transfers between devices with their start and end apart: 10, of which 3 were waited for; matrix products, arithmetic and copies ran while one was open for 22% of the time, Pallas kernels for 0%

profile of v1, /device:TPU:1, one launch (start us, length us, event | category | flops | bytes accessed | tf_op | source)
XLA Modules:
  0.0 237.3 jit_solution(6546082479456384387)
XLA Ops:
  6.5 1.7 reshape.874
  10.0 8.7 %collective-permute-start = (bf16[128,512]{1,0:T(8,128)(2,1)S(1)}, bf16[128,512]{1,0:T(8,128)(2,1)}, u32[]{:S(2)}, u32[]{:S(2)}) collective-permute-start(bf16[128,512]{1,0:T(8,128)(2,1)S(1)} %fusion.57), channel_id=1, source_target_pairs={{0,4},{4,0},{8,12},{12,8},{16,20},{20,16},{24,28},{28,24},{32,36},... | collective-permute-start | bytes 393224 | tf_op jit(solution)/shard_map/ppermute | solution.py:15
  21.8 1.9 collective-permute-start.1
  23.7 1.6 stack.2
  25.3 14.8 %all-to-all-start = ((bf16[128,512,16]{1,2,0:T(8,128)(2,1)}), bf16[128,512,16]{1,2,0:T(8,128)(2,1)}, u32[]{:S(2)}, u32[]{:S(2)}) async-start(bf16[128,512,16]{1,2,0:T(8,128)(2,1)} %stack.2), calls=%async_computation | async-start | bytes 4194304 | tf_op jit(solution)/shard_map/all_to_all | solution.py:152
  40.3 0.9 reshape.817
  41.2 0.9 reshape_reshape.9
  42.4 0.9 reshape.819
  50.5 1.1 convert_reduce_fusion.1
  54.4 1.0 fusion.1
  58.5 1.0 copy.252
  61.7 1.0 copy.257
  63.0 1.7 broadcast_select_fusion.9
  65.6 3.3 %collective-permute-start.3 = (bf16[128,512]{1,0:T(8,128)(2,1)S(1)}, bf16[128,512]{1,0:T(8,128)(2,1)S(1)}, u32[]{:S(2)}, u32[]{:S(2)}) collective-permute-start(bf16[128,512]{1,0:T(8,128)(2,1)S(1)} %fusion.55), channel_id=1, source_target_pairs={{0,8},{4,12},{8,0},{12,4},{16,24},{20,28},{24,16},{28,20},{32,40},... | collective-permute-start | bytes 393224 | tf_op jit(solution)/shard_map/ppermute | solution.py:15
  68.8 1.0 maximum_convert_fusion
  70.6 2.0 collective-permute-start.2
  72.6 60.6 %collective-permute-done.3 = bf16[128,512]{1,0:T(8,128)(2,1)S(1)} collective-permute-done((bf16[128,512]{1,0:T(8,128)(2,1)S(1)}, bf16[128,512]{1,0:T(8,128)(2,1)S(1)}, u32[]{:S(2)}, u32[]{:S(2)}) %collective-permute-start.3) | collective-permute-done | bytes 131104 | tf_op jit(solution)/shard_map/ppermute | solution.py:15
  134.1 4.2 %collective-permute-start.5 = (bf16[128,512]{1,0:T(8,128)(2,1)S(1)}, bf16[128,512]{1,0:T(8,128)(2,1)S(1)}, u32[]{:S(2)}, u32[]{:S(2)}) collective-permute-start(bf16[128,512]{1,0:T(8,128)(2,1)S(1)} %fusion.56), channel_id=1, source_target_pairs={{0,16},{4,20},{8,24},{12,28},{16,0},{20,4},{24,8},{28,12},{32,48},... | collective-permute-start | bytes 393224 | tf_op jit(solution)/shard_map/ppermute | solution.py:15
  138.3 1.0 copy.262
  139.4 1.1 fusion.121
  141.7 0.9 broadcast_select_fusion.7
  144.1 2.2 collective-permute-start.4
  146.3 1.0 copy.267
  150.2 7.0 %collective-permute-start.7 = (bf16[128,512]{1,0:T(8,128)(2,1)}, bf16[128,512]{1,0:T(8,128)(2,1)}, u32[]{:S(2)}, u32[]{:S(2)}) collective-permute-start(bf16[128,512]{1,0:T(8,128)(2,1)} %bitcast.274), channel_id=1, source_target_pairs={{0,32},{4,36},{8,40},{12,44},{16,48},{20,52},{24,56},{28,60},{32,0... | collective-permute-start | bytes 393224 | tf_op jit(solution)/shard_map/ppermute | solution.py:15
  157.2 1.0 copy.271
  160.2 1.0 broadcast_select_fusion.3
  162.2 4.3 %collective-permute-start.6 = (bf16[128,512]{1,0:T(8,128)(2,1)S(1)}, bf16[128,512]{1,0:T(8,128)(2,1)S(1)}, u32[]{:S(2)}, u32[]{:S(2)}) collective-permute-start(bf16[128,512]{1,0:T(8,128)(2,1)S(1)} %fusion.60), channel_id=1, source_target_pairs={{0,32},{4,36},{8,40},{12,44},{16,48},{20,52},{24,56},{28,60},{32,0... | collective-permute-start | bytes 393224 | tf_op jit(solution)/shard_map/ppermute | solution.py:15
  166.8 14.2 %collective-permute-done.6 = bf16[128,512]{1,0:T(8,128)(2,1)S(1)} collective-permute-done((bf16[128,512]{1,0:T(8,128)(2,1)S(1)}, bf16[128,512]{1,0:T(8,128)(2,1)S(1)}, u32[]{:S(2)}, u32[]{:S(2)}) %collective-permute-start.6) | collective-permute-done | bytes 131104 | tf_op jit(solution)/shard_map/ppermute | solution.py:15
  181.8 1.0 copy.283
  183.8 3.8 %fusion.13 = bf16[512,4,128]{2,0,1:T(8,128)(2,1)S(1)} fusion(f32[4,128,4,128]{3,1,0,2:T(8,128)S(1)} %copy.232, f32[512,4,128]{2,0,1:T(8,128)S(1)} %bitcast.275, f32[512,4,128]{2,0,1:T(8,128)S(1)} %bitcast.276, f32[512,4]{0,1:T(4,128)S(1)} %get-tuple-element.5, f32[512,4]{0,1:T(4,128)S(1)} %get-tuple-element.10, ...), kind=kLoop, calls=%fused_computation.27 | loop fusion | flops 4456448 | bytes 3989504 | tf_op jit(solution)/shard_map/convert_element_type | solution.py:147
  187.8 4.2 %convolution_convert_fusion = bf16[512,2048]{1,0:T(8,128)(2,1)} fusion(bf16[512,512]{0,1:T(8,128)(2,1)S(1)} %bitcast.285, bf16[512,2048]{0,1:T(8,128)(2,1)} %bitcast.79), kind=kOutput, calls=%fused_computation | convolution fusion | flops 1074790400 | bytes 4718592 | tf_op jit(solution)/shard_map/dot_general | solution.py:149
  192.0 38.4 %reduce-scatter.2.cloned.1.call-done = bf16[512,512]{1,0:T(8,128)(2,1)} async-done(((bf16[512,2048]{1,0:T(8,128)(2,1)}), bf16[512,512]{1,0:T(8,128)(2,1)}) %reduce-scatter.2.cloned.1.call-update) | async-done | bytes 524304 | tf_op jit(solution)/shard_map/reduce_scatter | solution.py:157
  (181 shorter events, 33.2 us)
Async XLA Ops:
  9.1 9.7 %copy-start.1 = (bf16[512,512]{1,0:T(8,128)(2,1)S(1)}, bf16[512,512]{1,0:T(8,128)(2,1)}, u32[]{:S(2)}) copy-start(bf16[512,512]{1,0:T(8,128)(2,1)} %param.6) | copy-start | bytes 1572868
  10.0 48.5 %collective-permute-start = (bf16[128,512]{1,0:T(8,128)(2,1)S(1)}, bf16[128,512]{1,0:T(8,128)(2,1)}, u32[]{:S(2)}, u32[]{:S(2)}) collective-permute-start(bf16[128,512]{1,0:T(8,128)(2,1)S(1)} %fusion.57), channel_id=1, source_target_pairs={{0,4},{4,0},{8,12},{12,8},{16,20},{20,16},{24,28},{28,24},{32,36},... | collective-permute-start | bytes 393224 | tf_op jit(solution)/shard_map/ppermute | solution.py:15
  20.2 3.5 %copy-start.27 = (bf16[512,16]{0,1:T(8,128)(2,1)S(1)}, bf16[512,16]{0,1:T(8,128)(2,1)}, u32[]{:S(2)}) copy-start(bf16[512,16]{0,1:T(8,128)(2,1)} %param.7) | copy-start | bytes 49156
  21.8 39.9 %collective-permute-start.1 = (bf16[128,512]{1,0:T(8,128)(2,1)}, bf16[128,512]{1,0:T(8,128)(2,1)}, u32[]{:S(2)}, u32[]{:S(2)}) collective-permute-start(bf16[128,512]{1,0:T(8,128)(2,1)} %fusion.54), channel_id=1, source_target_pairs={{0,4},{4,0},{8,12},{12,8},{16,20},{20,16},{24,28},{28,24},{32,36},... | collective-permute-start | bytes 393224 | tf_op jit(solution)/shard_map/ppermute | solution.py:15
  25.3 15.1 %copy-start = (bf16[512,512]{1,0:T(8,128)(2,1)S(1)}, bf16[512,512]{1,0:T(8,128)(2,1)}, u32[]{:S(2)}) copy-start(bf16[512,512]{1,0:T(8,128)(2,1)} %param.5) | copy-start | bytes 1572868
  25.3 162.5 %all-to-all-start = ((bf16[128,512,16]{1,2,0:T(8,128)(2,1)}), bf16[128,512,16]{1,2,0:T(8,128)(2,1)}, u32[]{:S(2)}, u32[]{:S(2)}) async-start(bf16[128,512,16]{1,2,0:T(8,128)(2,1)} %stack.2), calls=%async_computation | async-start | bytes 4194304 | tf_op jit(solution)/shard_map/all_to_all | solution.py:152
  40.1 2.3 copy-start.2
  40.1 190.3 %reduce-scatter.2.cloned.1.call-start = ((), (), s32[]{:S(2)}) async-start(), calls=%async_computation.2 | async-start | bytes 2621440 | tf_op jit(solution)/shard_map/reduce_scatter | solution.py:157
  44.8 2.1 copy-start.4
  44.8 3.0 %copy-start.3 = (bf16[2,2,128,4,128]{4,3,2,1,0:T(4,128)(2,1)S(1)}, bf16[2,2,128,4,128]{4,3,2,1,0:T(4,128)(2,1)}, u32[]{:S(2)}) copy-start(bf16[2,2,128,4,128]{4,3,2,1,0:T(4,128)(2,1)} %reshape_reshape.9) | copy-start | bytes 1572868
  49.8 3.1 %copy-start.6 = (bf16[1,2,128,4,128]{4,3,2,1,0:T(4,128)(2,1)S(1)}, bf16[1,2,128,4,128]{4,3,2,1,0:T(4,128)(2,1)}, u32[]{:S(2)}) copy-start(bf16[1,2,128,4,128]{4,3,2,1,0:T(4,128)(2,1)} %convert_element_type.255) | copy-start | bytes 786436
  49.8 3.2 %copy-start.7 = (bf16[2,128,4,128]{3,2,1,0:T(4,128)(2,1)S(1)}, bf16[2,128,4,128]{3,2,1,0:T(4,128)(2,1)}, u32[]{:S(2)}) copy-start(bf16[2,128,4,128]{3,2,1,0:T(4,128)(2,1)} %convert_element_type.253) | copy-start | bytes 786436
  65.6 67.7 %collective-permute-start.3 = (bf16[128,512]{1,0:T(8,128)(2,1)S(1)}, bf16[128,512]{1,0:T(8,128)(2,1)S(1)}, u32[]{:S(2)}, u32[]{:S(2)}) collective-permute-start(bf16[128,512]{1,0:T(8,128)(2,1)S(1)} %fusion.55), channel_id=1, source_target_pairs={{0,8},{4,12},{8,0},{12,4},{16,24},{20,28},{24,16},{28,20},{32,40},... | collective-permute-start | bytes 393224 | tf_op jit(solution)/shard_map/ppermute | solution.py:15
  70.6 67.8 %collective-permute-start.2 = (bf16[128,512]{1,0:T(8,128)(2,1)S(1)}, bf16[128,512]{1,0:T(8,128)(2,1)}, u32[]{:S(2)}, u32[]{:S(2)}) collective-permute-start(bf16[128,512]{1,0:T(8,128)(2,1)S(1)} %fusion.58), channel_id=1, source_target_pairs={{0,8},{4,12},{8,0},{12,4},{16,24},{20,28},{24,16},{28,20},{32,40},... | collective-permute-start | bytes 393224 | tf_op jit(solution)/shard_map/ppermute | solution.py:15
  134.1 14.1 %collective-permute-start.5 = (bf16[128,512]{1,0:T(8,128)(2,1)S(1)}, bf16[128,512]{1,0:T(8,128)(2,1)S(1)}, u32[]{:S(2)}, u32[]{:S(2)}) collective-permute-start(bf16[128,512]{1,0:T(8,128)(2,1)S(1)} %fusion.56), channel_id=1, source_target_pairs={{0,16},{4,20},{8,24},{12,28},{16,0},{20,4},{24,8},{28,12},{32,48},... | collective-permute-start | bytes 393224 | tf_op jit(solution)/shard_map/ppermute | solution.py:15
  142.6 5.0 %copy-start.15 = (f32[512,4]{0,1:T(4,128)S(1)}, f32[512,4]{0,1:T(4,128)}, u32[]{:S(2)}) copy-start(f32[512,4]{0,1:T(4,128)} %reshape.836) | copy-start | bytes 24580
  144.1 13.1 %collective-permute-start.4 = (bf16[128,512]{1,0:T(8,128)(2,1)}, bf16[128,512]{1,0:T(8,128)(2,1)}, u32[]{:S(2)}, u32[]{:S(2)}) collective-permute-start(bf16[128,512]{1,0:T(8,128)(2,1)} %fusion.59), channel_id=1, source_target_pairs={{0,16},{4,20},{8,24},{12,28},{16,0},{20,4},{24,8},{28,12},{32,48},... | collective-permute-start | bytes 393224 | tf_op jit(solution)/shard_map/ppermute | solution.py:15
  147.4 10.9 %copy-start.14 = (bf16[32,512]{1,0:T(8,128)(2,1)S(1)}, bf16[32,512]{1,0:T(8,128)(2,1)}, u32[]{:S(2)}) copy-start(bf16[32,512]{1,0:T(8,128)(2,1)} %get-tuple-element.16) | copy-start | bytes 98308
  150.2 31.7 %collective-permute-start.7 = (bf16[128,512]{1,0:T(8,128)(2,1)}, bf16[128,512]{1,0:T(8,128)(2,1)}, u32[]{:S(2)}, u32[]{:S(2)}) collective-permute-start(bf16[128,512]{1,0:T(8,128)(2,1)} %bitcast.274), channel_id=1, source_target_pairs={{0,32},{4,36},{8,40},{12,44},{16,48},{20,52},{24,56},{28,60},{32,0... | collective-permute-start | bytes 393224 | tf_op jit(solution)/shard_map/ppermute | solution.py:15
  158.5 2.8 %copy-start.18 = (f32[4,32]{1,0:T(4,128)}, f32[4,32]{1,0:T(4,128)S(1)}, u32[]{:S(2)}) copy-start(f32[4,32]{1,0:T(4,128)S(1)} %get-tuple-element.64) | copy-start | bytes 1540
  159.4 7.0 %copy-start.9 = (bf16[128,512]{1,0:T(8,128)(2,1)S(1)}, bf16[128,512]{1,0:T(8,128)(2,1)}, u32[]{:S(2)}) copy-start(bf16[128,512]{1,0:T(8,128)(2,1)} %copy-done.8) | copy-start | bytes 393220
  161.2 5.3 %copy-start.19 = (f32[4,32]{1,0:T(4,128)S(1)}, f32[4,32]{1,0:T(4,128)}, u32[]{:S(2)}) copy-start(f32[4,32]{1,0:T(4,128)} %copy-done.18) | copy-start | bytes 1540
  161.2 19.9 %copy-start.16 = (bf16[16,512]{1,0:T(8,128)(2,1)S(1)}, bf16[16,512]{1,0:T(8,128)(2,1)}, u32[]{:S(2)}) copy-start(bf16[16,512]{1,0:T(8,128)(2,1)} %convert_reduce_fusion.4) | copy-start | bytes 49156
  161.3 21.8 %copy-start.17 = (f32[4,4,128]{2,1,0:T(4,128)S(1)}, f32[4,4,128]{2,1,0:T(4,128)}, u32[]{:S(2)}) copy-start(f32[4,4,128]{2,1,0:T(4,128)} %fusion.1) | copy-start | bytes 24580
  161.6 21.5 %copy-start.20 = (f32[512,4]{0,1:T(4,128)S(1)}, f32[512,4]{0,1:T(4,128)}, u32[]{:S(2)}) copy-start(f32[512,4]{0,1:T(4,128)} %copy.286) | copy-start | bytes 24580
  161.6 21.5 %copy-start.21 = (f32[512,4]{0,1:T(4,128)S(1)}, f32[512,4]{0,1:T(4,128)}, u32[]{:S(2)}) copy-start(f32[512,4]{0,1:T(4,128)} %reshape.862) | copy-start | bytes 24580
  161.7 21.5 %copy-start.22 = (f32[512,4]{0,1:T(4,128)S(1)}, f32[512,4]{0,1:T(4,128)}, u32[]{:S(2)}) copy-start(f32[512,4]{0,1:T(4,128)} %reshape.864) | copy-start | bytes 24580
  161.7 21.5 %copy-start.23 = (f32[512,4]{0,1:T(4,128)S(1)}, f32[512,4]{0,1:T(4,128)}, u32[]{:S(2)}) copy-start(f32[512,4]{0,1:T(4,128)} %reshape.848) | copy-start | bytes 24580
  161.7 21.5 %copy-start.24 = (f32[512,4]{0,1:T(4,128)S(1)}, f32[512,4]{0,1:T(4,128)}, u32[]{:S(2)}) copy-start(f32[512,4]{0,1:T(4,128)} %reshape.866) | copy-start | bytes 24580
  161.7 21.5 %copy-start.25 = (f32[512,4]{0,1:T(4,128)S(1)}, f32[512,4]{0,1:T(4,128)}, u32[]{:S(2)}) copy-start(f32[512,4]{0,1:T(4,128)} %get-tuple-element.18) | copy-start | bytes 24580
  161.7 21.5 %copy-start.26 = (f32[512,4]{0,1:T(4,128)S(1)}, f32[512,4]{0,1:T(4,128)}, u32[]{:S(2)}) copy-start(f32[512,4]{0,1:T(4,128)} %get-tuple-element.19) | copy-start | bytes 24580
  162.2 18.8 %collective-permute-start.6 = (bf16[128,512]{1,0:T(8,128)(2,1)S(1)}, bf16[128,512]{1,0:T(8,128)(2,1)S(1)}, u32[]{:S(2)}, u32[]{:S(2)}) collective-permute-start(bf16[128,512]{1,0:T(8,128)(2,1)S(1)} %fusion.60), channel_id=1, source_target_pairs={{0,32},{4,36},{8,40},{12,44},{16,48},{20,52},{24,56},{28,60},{32,0... | collective-permute-start | bytes 393224 | tf_op jit(solution)/shard_map/ppermute | solution.py:15
  (6 other events, 8.4 us)
Sparse Core Ops, SparseCore 0:
  192.1 38.2 reduce-scatter.1
